TPU v7x, 512 devices: a whole 4x8x8 slice. The times are simulated.
512 devices in a mesh: context: 64 (over y, z), channel: 8 (over x, core).
Axes of the slice: x: 4, y: 8, z: 8, core: 2. Of those that a mesh axis runs over, the one named last changes fastest.
Arguments:
- inputs: bfloat16 [512, 32768], P('channel', 'context'), may hold values from -6 to 6
- grad_out: bfloat16 [512, 32768], P('channel', 'context'), may hold values from -36 to 36
- decay_rates: float32 [64, 16], replicated, as said below
- residues: float32 [64, 16], replicated, may hold values from -1.5 to 1.5
Outputs:
- grad_in: bfloat16 [512, 32768], P('channel', 'context')
- grad_residue: float32 [64, 16], replicated
- grad_log_rate: float32 [64, 16], replicated
Inputs may be any that keep to these rules, and one draw needn't show every extreme that they name: `decay_rates`: every rate lies between 0.3 / 32768 and 1 / 15.
All inputs are finite; a program needn't handle non-finite values.
Results may differ from a plain program's by a relative error of at most 0.001.
Values may be sent and summed in bfloat16 or wider, within the bound.
No kernel may reach another device: no remote copies, remote signals or barrier semaphores. Data moves between devices by JAX's collectives and lax.ppermute only.
A program may use at most 64 MiB of HBM per device.

v0:
```python
import math
import jax
import jax.numpy as jnp
from jax import lax
from jax.sharding import PartitionSpec as P

precise_setting = lax.Precision.HIGHEST


def forward_combine(earlier, later):
    decay_one, cross_one, state_one, slope_one = earlier
    decay_two, cross_two, state_two, second_slope = later
    return (
        decay_two * decay_one,
        decay_two * cross_one + cross_two * decay_one,
        decay_two * state_one + state_two,
        decay_two * slope_one + cross_two * state_one + second_slope,
    )


def backward_combine(earlier, later):
    decay_far, total_far = earlier
    decay_near, total_near = later
    return (decay_far * decay_near, total_near + decay_near * total_far)


def within_blocks(x_rows, g_rows, decay_rates, block_len):
    chan_count, pole_count = decay_rates.shape
    quarter = pole_count // 4
    offset = jnp.arange(block_len, dtype=jnp.float32)
    centre = float(block_len // 2)
    upper_ones = (offset[:, None] <= offset[None, :]).astype(jnp.float32)
    grouped = decay_rates.reshape(chan_count, 4, quarter).transpose(1, 0, 2)

    def one_group(rate_part):
        rate_col = rate_part[:, :, None]
        x_scaled = x_rows[:, None, :, :] * jnp.exp(-rate_col * (centre - offset))[:, :, None, :]
        g_scaled = g_rows[:, None, :, :] * jnp.exp(-rate_col * (offset - centre))[:, :, None, :]
        stacked = jnp.stack([x_scaled, x_scaled * offset], axis=2)
        running = jnp.einsum("nqsbv,vu->nqsbu", stacked, upper_ones, precision=precise_setting)
        first_part = jnp.sum(g_scaled * running[:, :, 0], axis=(2, 3))
        second_part = jnp.sum(
            g_scaled * (offset * running[:, :, 0] - running[:, :, 1]), axis=(2, 3)
        )
        return (first_part, second_part)

    first_all, second_all = lax.map(one_group, grouped)
    return (
        first_all.transpose(1, 0, 2).reshape(chan_count, pole_count),
        second_all.transpose(1, 0, 2).reshape(chan_count, pole_count),
    )


def prepare(inputs, grad_out, decay_rates, block_len):
    chan_count, length = inputs.shape
    blocks = length // block_len
    x_rows = inputs.astype(jnp.float32).reshape(chan_count, blocks, block_len)
    g_rows = grad_out.astype(jnp.float32).reshape(chan_count, blocks, block_len)
    offset = jnp.arange(block_len, dtype=jnp.float32)
    tail_pos = block_len - 1.0 - offset
    rate_col = decay_rates[:, :, None]
    tail_pow = jnp.exp(-rate_col * tail_pos)
    next_pow = jnp.exp(-rate_col * (offset + 1.0))
    x_weights = jnp.stack([tail_pow, tail_pos * tail_pow], axis=2)
    g_weights = jnp.stack(
        [next_pow, (offset + 1.0) * next_pow, jnp.exp(-rate_col * offset)], axis=2
    )
    x_ends = jnp.einsum("nbj,nksj->nksb", x_rows, x_weights, precision=precise_setting)
    g_ends = jnp.einsum("nbj,nksj->nksb", g_rows, g_weights, precision=precise_setting)
    block_decay = jnp.broadcast_to(
        jnp.exp(-decay_rates * block_len)[:, :, None], x_ends[:, :, 0].shape
    )
    forward = lax.associative_scan(
        forward_combine,
        (block_decay, block_len * block_decay, x_ends[:, :, 0], x_ends[:, :, 1]),
        axis=2,
    )
    backward = lax.associative_scan(
        backward_combine, (block_decay, g_ends[:, :, 2]), axis=2, reverse=True
    )
    first_in, second_in = within_blocks(x_rows, g_rows, decay_rates, block_len)
    return (g_rows, forward, backward, g_ends, first_in, second_in)


def complete(prepared, start_state, start_slope, end_adjoint, decay_rates, residues, block_len):
    g_rows, forward, backward, g_ends, first_in, second_in = prepared
    chan_count, blocks, _ = g_rows.shape
    unit_col = jnp.ones(decay_rates.shape + (1,), jnp.float32)
    zero_col = jnp.zeros_like(unit_col)
    lead_decay = jnp.concatenate([unit_col, forward[0][:, :, :-1]], axis=2)
    lead_cross = jnp.concatenate([zero_col, forward[1][:, :, :-1]], axis=2)
    lead_state = jnp.concatenate([zero_col, forward[2][:, :, :-1]], axis=2)
    lead_slope = jnp.concatenate([zero_col, forward[3][:, :, :-1]], axis=2)
    enter_state = lead_decay * start_state[:, :, None] + lead_state
    enter_slope = (
        lead_decay * start_slope[:, :, None] + lead_cross * start_state[:, :, None] + lead_slope
    )
    first_sum = first_in + jnp.sum(enter_state * g_ends[:, :, 0], axis=2)
    second_sum = second_in + jnp.sum(
        enter_slope * g_ends[:, :, 0] + enter_state * g_ends[:, :, 1], axis=2
    )
    decay_step = jnp.exp(-decay_rates)
    gain_pole = jnp.sqrt(-jnp.expm1(-2.0 * decay_rates))
    residue_gradient = gain_pole * first_sum
    log_grad = (
        residues
        * decay_rates
        * (decay_step * decay_step / gain_pole * first_sum - gain_pole * second_sum)
    )
    weighted = residues * gain_pole
    trail_decay = jnp.concatenate([backward[0][:, :, 1:], unit_col], axis=2)
    trail_total = jnp.concatenate([backward[1][:, :, 1:], zero_col], axis=2)
    incoming = (trail_total + trail_decay * end_adjoint[:, :, None]) * weighted[:, :, None]
    offset = jnp.arange(block_len, dtype=jnp.float32)
    centre = float(block_len // 2)
    rate_col = decay_rates[:, :, None]
    carried = jnp.einsum(
        "nkb,nkj->nbj",
        incoming,
        jnp.exp(-rate_col * (block_len - offset)),
        precision=precise_setting,
    )
    row_multiplier = weighted[:, :, None] * jnp.exp(-rate_col * (offset - centre))
    column_multiplier = jnp.exp(rate_col * (offset - centre))
    lower_mask = offset[:, None] >= offset[None, :]
    toeplitz = jnp.where(
        lower_mask[None],
        jnp.einsum("acr,acq->arq", row_multiplier, column_multiplier, precision=precise_setting),
        0.0,
    )
    local_part = jnp.einsum("nbu,nuv->nbv", g_rows, toeplitz, precision=precise_setting)
    grad_in = (local_part + carried).reshape(chan_count, blocks * block_len).astype(jnp.bfloat16)
    return (grad_in, residue_gradient, log_grad)


def body(inputs, grad_out, decay_rates, residues):
    chan_count, token_count = inputs.shape
    context_size = lax.axis_size("context")
    seq_total = token_count * context_size
    group_size = lax.axis_size("channel")
    pole_count = decay_rates.shape[1]
    zero_pair = jnp.zeros_like(decay_rates)
    share = chan_count // context_size
    moved_inputs, moved_grads = (
        lax.all_to_all(inputs, "context", split_axis=0, concat_axis=1, tiled=True),
        lax.all_to_all(grad_out, "context", split_axis=0, concat_axis=1, tiled=True),
    )
    first_row = lax.axis_index("context") * share
    my_rates = lax.dynamic_slice_in_dim(decay_rates, first_row, share, 0)
    my_residues = lax.dynamic_slice_in_dim(residues, first_row, share, 0)
    block_len = math.gcd(128, seq_total)
    prepared = prepare(moved_inputs, moved_grads, my_rates, block_len)
    zero_state = jnp.zeros((share, pole_count), jnp.float32)
    grad_part, res_part, log_part = complete(
        prepared, zero_state, zero_state, zero_state, my_rates, my_residues, block_len
    )
    grad_in = lax.all_to_all(grad_part, "context", split_axis=1, concat_axis=0, tiled=True)
    res_local = lax.dynamic_update_slice_in_dim(zero_pair, res_part, first_row, 0)
    log_local = lax.dynamic_update_slice_in_dim(zero_pair, log_part, first_row, 0)
    res_total, log_total = lax.psum((res_local, log_local), ("context", "channel"))
    norm_scale = 1.0 / math.sqrt(seq_total * group_size)
    return (grad_in, res_total * norm_scale, log_total * norm_scale)


def solution(mesh):
    return jax.shard_map(
        body,
        mesh=mesh,
        in_specs=(P("channel", "context"), P("channel", "context"), P(), P()),
        out_specs=(P("channel", "context"), P(), P()),
        check_vma=False,
    )
```

profile of v0, /device:TPU:1, one launch (start us, length us, event | category | flops | bytes accessed | tf_op | source)
XLA Modules:
  0.0 199.6 jit_solution(9558295038052606538)
XLA Ops:
  1.1 1.5 reduce.24
  2.6 0.6 reshape.1135
  3.3 17.3 %all-to-all-start.2 = ((bf16[64,2,256]{2,1,0:T(2,128)(2,1)}), bf16[64,2,256]{2,1,0:T(2,128)(2,1)S(1)}, u32[]{:S(2)}, u32[]{:S(2)}) async-start(bf16[64,2,256]{2,1,0:T(2,128)(2,1)} %reshape.1135), calls=%async_computation.2 | async-start | bytes 131072 | tf_op jit(solution)/shard_map/all_to_all | solution.py:145
  20.6 0.7 copy-done.1
  22.4 0.7 reduce.25
  23.1 0.6 reshape.1131
  23.7 7.9 %all-to-all-done.2 = bf16[64,2,256]{2,1,0:T(2,128)(2,1)S(1)} async-done(((bf16[64,2,256]{2,1,0:T(2,128)(2,1)}), bf16[64,2,256]{2,1,0:T(2,128)(2,1)S(1)}, u32[]{:S(2)}, u32[]{:S(2)}) %all-to-all-start.2) | async-done | bytes 65568 | tf_op jit(solution)/shard_map/all_to_all | solution.py:145
  31.7 4.8 %all-to-all-start = ((bf16[64,2,256]{2,1,0:T(2,128)(2,1)}), bf16[64,2,256]{2,1,0:T(2,128)(2,1)S(1)}, u32[]{:S(2)}, u32[]{:S(2)}) async-start(bf16[64,2,256]{2,1,0:T(2,128)(2,1)} %reshape.1131), calls=%async_computation | async-start | bytes 131072 | tf_op jit(solution)/shard_map/all_to_all | solution.py:146
  43.7 3.7 %all-to-all-done = bf16[64,2,256]{2,1,0:T(2,128)(2,1)S(1)} async-done(((bf16[64,2,256]{2,1,0:T(2,128)(2,1)}), bf16[64,2,256]{2,1,0:T(2,128)(2,1)S(1)}, u32[]{:S(2)}, u32[]{:S(2)}) %all-to-all-start) | async-done | bytes 65568 | tf_op jit(solution)/shard_map/all_to_all | solution.py:146
  68.6 6.0 %while.16 = (s32[]{:T(128)}, f32[4,1,4]{2,1,0:T(1,128)S(1)}, f32[4,1,4]{2,1,0:T(1,128)S(1)}, f32[1,32768]{1,0:T(1,128)S(1)}, f32[4,1,4]{2,1,0:T(1,128)S(1)}, /*index=5*/f32[1,32768]{1,0:T(1,128)S(1)}, s32[]{:T(128)}) while((s32[]{:T(128)}, f32[4,1,4]{2,1,0:T(1,128)S(1)}, f32[4,1,4]{2,1,0:T(1,128)S(1)}, ...), condition=%wide.region_3.4_spmd.clone.clone, body=%wide.region_0.3_spmd.clone.clone.sunk | while | flops 404129024 | bytes 4468909 | solution.py:47
  69.0 1.0 convolution_bitcast_fusion.5
  70.4 1.0 convolution_bitcast_fusion.5
  71.9 1.0 convolution_bitcast_fusion.5
  73.3 1.0 convolution_bitcast_fusion.5
  75.1 0.7 reduce.22
  75.8 0.7 reduce.21
  80.1 96.9 %all-reduce.102 = (f32[64,16]{0,1:T(8,128)S(1)}, f32[64,16]{0,1:T(8,128)S(1)}) all-reduce(f32[64,16]{0,1:T(8,128)S(1)} %dynamic_update_slice.19, f32[64,16]{0,1:T(8,128)S(1)} %dynamic_update_slice.20), channel_id=1, replica_groups=mesh['context'=64,'channel'=8] {'context','channel'}, use_global_device_ids=true, to_apply=%region_5.6 | all-reduce | flops 2048 | bytes 16384 | tf_op jit(solution)/shard_map/psum | solution.py:160
  177.0 0.6 broadcast_multiply_fusion.3
  178.8 1.0 reduce.26
  179.8 0.6 reshape.1133
  180.5 7.2 %all-to-all-start.1 = ((bf16[64,2,256]{2,1,0:T(2,128)(2,1)}), bf16[64,2,256]{2,1,0:T(2,128)(2,1)S(1)}, u32[]{:S(2)}, u32[]{:S(2)}) async-start(bf16[64,2,256]{2,1,0:T(2,128)(2,1)} %reshape.1133), calls=%async_computation.1 | async-start | bytes 131072 | tf_op jit(solution)/shard_map/all_to_all | solution.py:157
  187.7 0.6 broadcast_multiply_fusion.2
  188.3 10.5 %all-to-all-done.1 = bf16[64,2,256]{2,1,0:T(2,128)(2,1)S(1)} async-done(((bf16[64,2,256]{2,1,0:T(2,128)(2,1)}), bf16[64,2,256]{2,1,0:T(2,128)(2,1)S(1)}, u32[]{:S(2)}, u32[]{:S(2)}) %all-to-all-start.1) | async-done | bytes 65568 | tf_op jit(solution)/shard_map/all_to_all | solution.py:157
  198.9 0.6 copy.204
  (375 shorter events, 36.1 us)
Async XLA Ops:
  3.3 17.3 %copy-start.2 = (f32[64,16]{0,1:T(8,128)S(1)}, f32[64,16]{0,1:T(8,128)}, u32[]{:S(2)}) copy-start(f32[64,16]{0,1:T(8,128)} %param.9) | copy-start | bytes 12292
  3.3 28.4 %all-to-all-start.2 = ((bf16[64,2,256]{2,1,0:T(2,128)(2,1)}), bf16[64,2,256]{2,1,0:T(2,128)(2,1)S(1)}, u32[]{:S(2)}, u32[]{:S(2)}) async-start(bf16[64,2,256]{2,1,0:T(2,128)(2,1)} %reshape.1135), calls=%async_computation.2 | async-start | bytes 131072 | tf_op jit(solution)/shard_map/all_to_all | solution.py:145
  20.6 0.7 copy-start.1
  21.6 0.8 copy-start
  31.7 15.7 %all-to-all-start = ((bf16[64,2,256]{2,1,0:T(2,128)(2,1)}), bf16[64,2,256]{2,1,0:T(2,128)(2,1)S(1)}, u32[]{:S(2)}, u32[]{:S(2)}) async-start(bf16[64,2,256]{2,1,0:T(2,128)(2,1)} %reshape.1131), calls=%async_computation | async-start | bytes 131072 | tf_op jit(solution)/shard_map/all_to_all | solution.py:146
  180.5 18.4 %all-to-all-start.1 = ((bf16[64,2,256]{2,1,0:T(2,128)(2,1)}), bf16[64,2,256]{2,1,0:T(2,128)(2,1)S(1)}, u32[]{:S(2)}, u32[]{:S(2)}) async-start(bf16[64,2,256]{2,1,0:T(2,128)(2,1)} %reshape.1133), calls=%async_computation.1 | async-start | bytes 131072 | tf_op jit(solution)/shard_map/all_to_all | solution.py:157
where the time goes:
time: 200 us
  blocking collectives  96.9 us (48%)
  local copies, waits for them, and re-layouts  29.6 us (15%)
  starting transfers between devices  29.3 us (15%)
  waiting for transfers between devices  22.1 us (11%)
  other arithmetic  14.1 us (7%)
  matrix products  5.37 us (3%)
    psum x1, blocking collectives, body(): lax.psum((res_local, log_local), ('context', 'channel'))  96.9 us
    all_to_all x1, starting transfers between devices, body(): lax.all_to_all(inputs, 'context', split_axis=0, concat_axis=1, tiled=True)  17.3 us
    all_to_all x1, waiting for transfers between devices, body(): lax.all_to_all(grad_part, 'context', split_axis=1, concat_axis=0, tiled=T...  10.5 us
    all_to_all x1, waiting for transfers between devices, body(): lax.all_to_all(inputs, 'context', split_axis=0, concat_axis=1, tiled=True)  7.95 us
    all_to_all x1, starting transfers between devices, body(): lax.all_to_all(grad_part, 'context', split_axis=1, concat_axis=0, tiled=T...  7.24 us
    unnamed x26, local copies, waits for them, and re-layouts  6.29 us
    slice x43, local copies, waits for them, and re-layouts, prepare(): lax.associative_scan(forward_combine, (block_decay, block_len * block_dec...  6.06 us
    slice x46, local copies, waits for them, and re-layouts, prepare(): lax.associative_scan(backward_combine, (block_decay, g_ends[:, :, 2]), ax...  5.62 us
  transfers between devices with their start and end apart: 3, of which 3 were waited for; matrix products, arithmetic and copies ran while one was open for 5% of the time, Pallas kernels for 0%

commit v1 on v0

--- a/solution.py
+++ b/solution.py
@@ -157,7 +157,7 @@
     grad_in = lax.all_to_all(grad_part, "context", split_axis=1, concat_axis=0, tiled=True)
     res_local = lax.dynamic_update_slice_in_dim(zero_pair, res_part, first_row, 0)
     log_local = lax.dynamic_update_slice_in_dim(zero_pair, log_part, first_row, 0)
-    res_total, log_total = lax.psum((res_local, log_local), ("context", "channel"))
+    res_total, log_total = lax.psum(lax.psum((res_local, log_local), "context"), "channel")
     norm_scale = 1.0 / math.sqrt(seq_total * group_size)
     return (grad_in, res_total * norm_scale, log_total * norm_scale)
 

time: 200 us -> 401 us (2.00)
  blocking collectives: 96.9 us -> 298 us
    psum x1 -> x2, blocking collectives: 96.9 us -> 298 us  [the longest x1 220 us: body(): lax.psum((res_local, log_local), 'context')]
  transfers between devices with their start and end apart: 3 -> 3, of which waited for: 3 -> 3; matrix products, arithmetic and copies ran while one was open for 5% -> 3% of each run, Pallas kernels for 0% -> 0%
where the time goes in v1:
time: 401 us; the launch traced here: 398 us
  blocking collectives  298 us (74%)
  local copies, waits for them, and re-layouts  29.6 us (7%)
  starting transfers between devices  26.9 us (7%)
  waiting for transfers between devices  22.1 us (6%)
  other arithmetic  14.1 us (4%)
  matrix products  5.37 us (1%)
    psum x1, blocking collectives, body(): lax.psum((res_local, log_local), 'context')  220 us
    psum x1, blocking collectives, body(): lax.psum(lax.psum((res_local, log_local), 'context'), 'channel')  77.6 us
    all_to_all x1, starting transfers between devices, body(): lax.all_to_all(inputs, 'context', split_axis=0, concat_axis=1, tiled=True)  17.3 us
    all_to_all x1, waiting for transfers between devices, body(): lax.all_to_all(grad_part, 'context', split_axis=1, concat_axis=0, tiled=T...  10.5 us
  transfers between devices with their start and end apart: 3, of which 3 were waited for; matrix products, arithmetic and copies ran while one was open for 3% of the time, Pallas kernels for 0%

profile of v1, /device:TPU:1, one launch (start us, length us, event | category | flops | bytes accessed | tf_op | source)
XLA Modules:
  0.0 398.1 jit_solution(1085533768989655288)
XLA Ops:
  1.1 1.5 reduce.24
  2.6 0.6 reshape.1135
  3.3 17.3 %all-to-all-start.2 = ((bf16[64,2,256]{2,1,0:T(2,128)(2,1)}), bf16[64,2,256]{2,1,0:T(2,128)(2,1)S(1)}, u32[]{:S(2)}, u32[]{:S(2)}) async-start(bf16[64,2,256]{2,1,0:T(2,128)(2,1)} %reshape.1135), calls=%async_computation.2 | async-start | bytes 131072 | tf_op jit(solution)/shard_map/all_to_all | solution.py:145
  20.6 0.7 copy-done.1
  22.4 0.7 reduce.25
  23.1 0.6 reshape.1131
  23.7 8.0 %all-to-all-done.2 = bf16[64,2,256]{2,1,0:T(2,128)(2,1)S(1)} async-done(((bf16[64,2,256]{2,1,0:T(2,128)(2,1)}), bf16[64,2,256]{2,1,0:T(2,128)(2,1)S(1)}, u32[]{:S(2)}, u32[]{:S(2)}) %all-to-all-start.2) | async-done | bytes 65568 | tf_op jit(solution)/shard_map/all_to_all | solution.py:145
  31.7 4.8 %all-to-all-start = ((bf16[64,2,256]{2,1,0:T(2,128)(2,1)}), bf16[64,2,256]{2,1,0:T(2,128)(2,1)S(1)}, u32[]{:S(2)}, u32[]{:S(2)}) async-start(bf16[64,2,256]{2,1,0:T(2,128)(2,1)} %reshape.1131), calls=%async_computation | async-start | bytes 131072 | tf_op jit(solution)/shard_map/all_to_all | solution.py:146
  43.7 3.7 all-to-all-done
  68.5 6.0 %while.16 = (s32[]{:T(128)}, f32[4,1,4]{2,1,0:T(1,128)S(1)}, f32[4,1,4]{2,1,0:T(1,128)S(1)}, f32[1,32768]{1,0:T(1,128)S(1)}, f32[4,1,4]{2,1,0:T(1,128)S(1)}, /*index=5*/f32[1,32768]{1,0:T(1,128)S(1)}, s32[]{:T(128)}) while((s32[]{:T(128)}, f32[4,1,4]{2,1,0:T(1,128)S(1)}, f32[4,1,4]{2,1,0:T(1,128)S(1)}, ...), condition=%wide.region_3.4_spmd.clone.clone, body=%wide.region_0.3_spmd.clone.clone.sunk | while | flops 404129024 | bytes 4468909 | solution.py:47
  69.0 1.0 convolution_bitcast_fusion.5
  70.4 1.0 convolution_bitcast_fusion.5
  71.8 1.0 convolution_bitcast_fusion.5
  73.3 1.0 convolution_bitcast_fusion.5
  75.0 0.7 reduce.22
  75.8 0.7 reduce.21
  80.1 220.3 %all-reduce.102 = (f32[64,16]{0,1:T(8,128)S(1)}, f32[64,16]{0,1:T(8,128)S(1)}) all-reduce(f32[64,16]{0,1:T(8,128)S(1)} %dynamic_update_slice.19, f32[64,16]{0,1:T(8,128)S(1)} %dynamic_update_slice.20), channel_id=1, replica_groups=mesh['context'=64,'channel'=8] {'context'}, use_global_device_ids=true, to_apply=%region_5.6 | all-reduce | flops 2048 | bytes 16384 | tf_op jit(solution)/shard_map/psum | solution.py:160
  300.4 77.6 %all-reduce.103 = (f32[64,16]{0,1:T(8,128)S(1)}, f32[64,16]{0,1:T(8,128)S(1)}) all-reduce(f32[64,16]{0,1:T(8,128)S(1)} %get-tuple-element.205, f32[64,16]{0,1:T(8,128)S(1)} %get-tuple-element.206), channel_id=1, replica_groups=mesh['context'=64,'channel'=8] {'channel'}, use_global_device_ids=true, to_apply=%region_6.7 | all-reduce | flops 2048 | bytes 16384 | tf_op jit(solution)/shard_map/psum | solution.py:160
  379.8 1.0 reduce.26
  380.8 0.6 reshape.1133
  381.4 4.9 %all-to-all-start.1 = ((bf16[64,2,256]{2,1,0:T(2,128)(2,1)}), bf16[64,2,256]{2,1,0:T(2,128)(2,1)S(1)}, u32[]{:S(2)}, u32[]{:S(2)}) async-start(bf16[64,2,256]{2,1,0:T(2,128)(2,1)} %reshape.1133), calls=%async_computation.1 | async-start | bytes 131072 | tf_op jit(solution)/shard_map/all_to_all | solution.py:157
  386.3 0.6 broadcast_multiply_fusion.2
  386.9 10.5 %all-to-all-done.1 = bf16[64,2,256]{2,1,0:T(2,128)(2,1)S(1)} async-done(((bf16[64,2,256]{2,1,0:T(2,128)(2,1)}), bf16[64,2,256]{2,1,0:T(2,128)(2,1)S(1)}, u32[]{:S(2)}, u32[]{:S(2)}) %all-to-all-start.1) | async-done | bytes 65568 | tf_op jit(solution)/shard_map/all_to_all | solution.py:157
  397.5 0.6 copy.204
  (376 shorter events, 36.7 us)
Async XLA Ops:
  3.3 17.3 %copy-start.2 = (f32[64,16]{0,1:T(8,128)S(1)}, f32[64,16]{0,1:T(8,128)}, u32[]{:S(2)}) copy-start(f32[64,16]{0,1:T(8,128)} %param.9) | copy-start | bytes 12292
  3.3 28.4 %all-to-all-start.2 = ((bf16[64,2,256]{2,1,0:T(2,128)(2,1)}), bf16[64,2,256]{2,1,0:T(2,128)(2,1)S(1)}, u32[]{:S(2)}, u32[]{:S(2)}) async-start(bf16[64,2,256]{2,1,0:T(2,128)(2,1)} %reshape.1135), calls=%async_computation.2 | async-start | bytes 131072 | tf_op jit(solution)/shard_map/all_to_all | solution.py:145
  20.6 0.7 copy-start.1
  21.6 0.8 copy-start
  31.7 15.7 %all-to-all-start = ((bf16[64,2,256]{2,1,0:T(2,128)(2,1)}), bf16[64,2,256]{2,1,0:T(2,128)(2,1)S(1)}, u32[]{:S(2)}, u32[]{:S(2)}) async-start(bf16[64,2,256]{2,1,0:T(2,128)(2,1)} %reshape.1131), calls=%async_computation | async-start | bytes 131072 | tf_op jit(solution)/shard_map/all_to_all | solution.py:146
  381.4 16.0 %all-to-all-start.1 = ((bf16[64,2,256]{2,1,0:T(2,128)(2,1)}), bf16[64,2,256]{2,1,0:T(2,128)(2,1)S(1)}, u32[]{:S(2)}, u32[]{:S(2)}) async-start(bf16[64,2,256]{2,1,0:T(2,128)(2,1)} %reshape.1133), calls=%async_computation.1 | async-start | bytes 131072 | tf_op jit(solution)/shard_map/all_to_all | solution.py:157
